TPU v7x, 128 devices: a whole 4x4x4 slice. The times are simulated.
128 devices in a mesh: sample: 4 (over z), marker: 32 (over y, x, core).
Axes of the slice: x: 4, y: 4, z: 4, core: 2. Of those that a mesh axis runs over, the one named last changes fastest.
Arguments:
- genotypes: bfloat16 [8192, 131072], P('sample', 'marker'), may hold values from -6 to 6
- phenotypes: float32 [16, 8192], P(None, 'sample'), may hold values from -6 to 6
- message: float32 [16, 131072], P(None, 'marker'), may hold values from -6 to 6
- probes: float32 [112, 131072], P(None, 'marker'), may hold values from -16 to 16
- inclusion: float32 [16], replicated, may hold values from 0.3 to 0.6
- slab_ratio: float32 [16], replicated, may hold values from 0.25 to 0.67
- input_precision: float32 [16], replicated, may hold values from 0.5 to 2
- noise_precision: float32 [16], replicated, may hold values from 4 to 16
Outputs:
- estimate: float32 [16, 131072], P(None, 'marker')
- lmmse_estimate: float32 [16, 131072], P(None, 'marker')
All inputs are finite; a program needn't handle non-finite values.
Results may differ from a plain program's by a relative error of at most 0.0013.
Values may be sent and summed in bfloat16 or wider, within the bound.
A program may use at most 128 MiB of HBM per device.

v0:
```python
import jax
import jax.numpy as jnp
from jax import lax
from jax.sharding import PartitionSpec as P

MARKERS = 131072
ITERS = 2


def denoise(signal, precision, shrink, logit_base):
    energy = shrink * precision * signal * signal
    weight = jax.nn.sigmoid(logit_base + 0.5 * energy)
    return (shrink * weight * signal, shrink * weight * (1.0 + (1.0 - weight) * energy))


def contract_rows(vectors, genotypes):
    return lax.dot_general(
        vectors, genotypes, (((1,), (1,)), ((), ())), preferred_element_type=jnp.float32
    )


def project(vectors_b, genotypes, offset):
    partial_value = contract_rows(vectors_b, genotypes)
    predicted = lax.psum(partial_value, "marker")
    if offset is not None:
        predicted = offset - predicted
    predicted_b = predicted.astype(jnp.bfloat16)
    widened = predicted_b.astype(jnp.float32)
    back_sum = jnp.dot(predicted_b, genotypes, preferred_element_type=jnp.float32)
    return (back_sum, jnp.sum(widened * widened, axis=1))


def per_device(
    genotypes, phenotypes, message, probes, inclusion, slab_ratio, input_precision, noise_precision
):
    people = genotypes.shape[0] * lax.axis_size("sample")
    traits = message.shape[0]
    copies = probes.shape[0] // traits + 1
    shrink = (slab_ratio / (1.0 + slab_ratio))[:, None]
    odds = jnp.log(inclusion / (1.0 - inclusion))[:, None]
    logit_base = odds + 0.5 * jnp.log(1.0 - shrink)
    first, slopes = denoise(message, input_precision[:, None], shrink, logit_base)
    first_slope = lax.psum(jnp.sum(slopes, axis=1), "marker") / MARKERS
    second_precision = input_precision * (1.0 - first_slope) / first_slope
    centre = (first - first_slope[:, None] * message) / (1.0 - first_slope)[:, None]
    start_back, unused_square = project(centre.astype(jnp.bfloat16), genotypes, phenotypes)
    start_back = lax.psum(start_back, "sample")
    start_res = noise_precision[:, None] / people * start_back
    scale_col = jnp.tile(noise_precision / people, copies)[:, None]
    prec_col = jnp.tile(second_precision, copies)[:, None]
    iterate = jnp.concatenate([centre, jnp.zeros(probes.shape, jnp.float32)], axis=0)
    residual = jnp.concatenate([start_res, probes], axis=0)
    direction = residual
    norm_start = lax.psum(jnp.sum(residual * residual, axis=1), "marker")
    norm_now = norm_start
    for iteration in range(ITERS):
        back_sum, square = project(direction.astype(jnp.bfloat16), genotypes, None)
        back_sum = lax.psum(back_sum, "sample")
        applied = scale_col * back_sum + prec_col * direction
        curvature = lax.psum(jnp.sum(direction * applied, axis=1), "marker")
        step_size = norm_now / curvature
        iterate = iterate + step_size[:, None] * direction
        if iteration + 1 < ITERS:
            residual = residual - step_size[:, None] * applied
            norm_next = lax.psum(jnp.sum(residual * residual, axis=1), "marker")
            beta_ratio = norm_next / norm_now
            direction = residual + beta_ratio[:, None] * direction
            norm_now = norm_next
    lmmse_estimate = iterate[:traits]
    probe_local = jnp.sum(
        jnp.sum(probes * iterate[traits:], axis=1).reshape(copies - 1, traits), axis=0
    )
    probe_dot = lax.psum(probe_local, "marker")
    probe_norm = jnp.sum(norm_start[traits:].reshape(copies - 1, traits), axis=0)
    second_slope = second_precision * probe_dot / (probe_norm + 1e-06)
    next_precision = second_precision * (1.0 - second_slope) / second_slope
    next_message = (lmmse_estimate - second_slope[:, None] * centre) / (1.0 - second_slope)[:, None]
    slab_var = slab_ratio / input_precision
    next_shrink = (slab_var * next_precision / (1.0 + slab_var * next_precision))[:, None]
    next_base = odds + 0.5 * jnp.log(1.0 - next_shrink)
    estimate, unused_slopes = denoise(next_message, next_precision[:, None], next_shrink, next_base)
    return (estimate, lmmse_estimate)


def solution(mesh):
    return jax.shard_map(
        per_device,
        mesh=mesh,
        in_specs=(
            P("sample", "marker"),
            P(None, "sample"),
            P(None, "marker"),
            P(None, "marker"),
            P(),
            P(),
            P(),
            P(),
        ),
        out_specs=(P(None, "marker"), P(None, "marker")),
        check_vma=False,
    )
```

profile of v0, /device:TPU:1, one launch (start us, length us, event | category | flops | bytes accessed | tf_op | source)
XLA Modules:
  0.0 946.0 jit_solution(1127837189394486947)
XLA Ops:
  7.2 0.0 all-reduce.9.cloned.1.call-start
  7.2 0.7 multiply_add_fusion.4
  7.9 0.7 mul.192
  8.6 1.3 multiply_reduce_fusion.4
  9.8 63.8 %psum.84 = f32[16]{0:T(128)S(1)} all-reduce(f32[16]{0:T(128)S(1)} %multiply_reduce_fusion.4), channel_id=1, replica_groups=mesh['sample'=4,'marker'=32] {'marker'}, use_global_device_ids=true, to_apply=%region_1.0 | all-reduce | flops 16 | bytes 128 | tf_op jit(solution)/shard_map/psum | solution.py:43
  73.6 0.7 multiply_divide_fusion.1
  74.3 1.1 subtract_divide_fusion
  75.4 0.0 copy-start.3
  75.4 10.9 %fusion.17 = f32[16,2048]{1,0:T(8,128)} fusion(bf16[2048,4096]{1,0:T(8,128)(2,1)} %param.8, f32[16,4096]{1,0:T(8,128)S(1)} %subtract_divide_fusion), kind=kOutput, calls=%fused_computation.33 | convolution fusion | flops 268500992 | bytes 17170432 | tf_op jit(solution)/shard_map/dot_general | solution.py:17
  86.3 0.0 all-reduce.9.cloned.1.call-update
  86.3 0.0 copy-start.6
  86.3 0.0 copy-start
  86.4 0.0 all-reduce.11.cloned.1.call-start
  86.4 102.7 %all-reduce.9.cloned.1.call-done = f32[16,2048]{1,0:T(8,128)} async-done(((f32[16,2048]{1,0:T(8,128)}), f32[16,2048]{1,0:T(8,128)}) %all-reduce.9.cloned.1.call-update) | async-done | bytes 131088 | tf_op jit(solution)/shard_map/psum | solution.py:24
  189.1 0.0 copy-done.3
  189.1 8.8 fusion.19
  197.9 0.0 all-reduce.11.cloned.1.call-update
  197.9 0.0 all-reduce.13.cloned.1.call-start
  198.0 0.0 copy-done.6
  198.0 39.8 %all-reduce.11.cloned.1.call-done = f32[16,4096]{1,0:T(8,128)} async-done(((f32[16,4096]{1,0:T(8,128)}), f32[16,4096]{1,0:T(8,128)}) %all-reduce.11.cloned.1.call-update) | async-done | bytes 262160 | tf_op jit(solution)/shard_map/psum | solution.py:47
  237.8 1.0 broadcast_multiply_fusion
  238.8 0.0 copy-done
  238.8 11.4 %fusion.3 = f32[128,2048]{1,0:T(8,128)S(1)} fusion(bf16[2048,4096]{1,0:T(8,128)(2,1)} %param.8, f32[112,4096]{1,0:T(8,128)S(1)} %copy-done, f32[16,4096]{1,0:T(8,128)S(1)} %broadcast_multiply_fusion), kind=kOutput, calls=%fused_computation.13 | convolution fusion | flops 2149580800 | bytes 19922944 | tf_op jit(solution)/shard_map/dot_general | solution.py:17
  250.2 134.0 %all-reduce.16 = bf16[128,2048]{1,0:T(8,128)(2,1)} all-reduce(f32[128,2048]{1,0:T(8,128)S(1)} %fusion.3), channel_id=1, replica_groups=mesh['sample'=4,'marker'=32] {'marker'}, use_global_device_ids=true, to_apply=%region_6.0 | all-reduce | flops 262144 | bytes 1572864 | tf_op jit(solution)/shard_map/psum | solution.py:24
  384.2 9.6 %fusion.24 = f32[128,4096]{1,0:T(8,128)} fusion(bf16[128,2048]{1,0:T(8,128)(2,1)} %all-reduce.16, bf16[2048,4096]{1,0:T(8,128)(2,1)} %param.8), kind=kOutput, calls=%fused_computation.52 | convolution fusion | flops 2147483648 | bytes 19398656 | tf_op jit(solution)/shard_map/dot_general | solution.py:29
  393.9 0.0 all-reduce.13.cloned.1.call-update
  393.9 0.0 all-reduce.15.cloned.1.call-start
  394.0 0.1 mul.210
  394.0 0.1 mul.207
  394.1 59.5 %all-reduce.13.cloned.1.call-done = f32[128,4096]{1,0:T(8,128)} async-done(((f32[128,4096]{1,0:T(8,128)}), f32[128,4096]{1,0:T(8,128)}) %all-reduce.13.cloned.1.call-update) | async-done | bytes 2097168 | tf_op jit(solution)/shard_map/psum | solution.py:58
  453.6 2.2 multiply_reduce_fusion.2
  455.8 62.9 %all-reduce.1 = (f32[128]{0:T(128)S(1)}, f32[128]{0:T(128)S(1)}) all-reduce(f32[128]{0:T(128)S(1)} %get-tuple-element.3, f32[128]{0:T(128)S(1)} %get-tuple-element.2), channel_id=1, replica_groups=mesh['sample'=4,'marker'=32] {'marker'}, use_global_device_ids=true, to_apply=%region_5.0 | all-reduce | flops 256 | bytes 2048 | tf_op jit(solution)/shard_map/psum | solution.py:54
  518.7 2.2 multiply_reduce_fusion.1
  520.9 66.8 %psum.91 = f32[128]{0:T(128)S(1)} all-reduce(f32[128]{0:T(128)S(1)} %multiply_reduce_fusion.1), channel_id=1, replica_groups=mesh['sample'=4,'marker'=32] {'marker'}, use_global_device_ids=true, to_apply=%region_11.0 | all-reduce | flops 128 | bytes 1024 | tf_op jit(solution)/shard_map/psum | solution.py:65
  587.7 3.6 multiply_add_fusion.1
  591.3 12.1 %fusion.1 = f32[128,2048]{1,0:T(8,128)S(1)} fusion(bf16[2048,4096]{1,0:T(8,128)(2,1)} %param.8, f32[128,4096]{1,0:T(8,128)} %multiply_add_fusion.1), kind=kOutput, calls=%fused_computation.11 | convolution fusion | flops 2148007936 | bytes 19922944 | tf_op jit(solution)/shard_map/dot_general | solution.py:17
  603.4 129.5 %all-reduce.17 = bf16[128,2048]{1,0:T(8,128)(2,1)} all-reduce(f32[128,2048]{1,0:T(8,128)S(1)} %fusion.1), channel_id=1, replica_groups=mesh['sample'=4,'marker'=32] {'marker'}, use_global_device_ids=true, to_apply=%region_12.0 | all-reduce | flops 262144 | bytes 1572864 | tf_op jit(solution)/shard_map/psum | solution.py:24
  732.9 9.6 %fusion.23 = f32[128,4096]{1,0:T(8,128)} fusion(bf16[128,2048]{1,0:T(8,128)(2,1)} %all-reduce.17, bf16[2048,4096]{1,0:T(8,128)(2,1)} %param.8), kind=kOutput, calls=%fused_computation.51 | convolution fusion | flops 2147483648 | bytes 19398656 | tf_op jit(solution)/shard_map/dot_general | solution.py:29
  742.5 0.0 all-reduce.15.cloned.1.call-update
  742.5 0.1 slice.18
  742.6 0.1 reshape.48
  742.7 58.7 %all-reduce.15.cloned.1.call-done = f32[128,4096]{1,0:T(8,128)} async-done(((f32[128,4096]{1,0:T(8,128)}), f32[128,4096]{1,0:T(8,128)}) %all-reduce.15.cloned.1.call-update) | async-done | bytes 2097168 | tf_op jit(solution)/shard_map/psum | solution.py:58
  801.3 2.7 multiply_reduce_fusion
  804.1 62.9 %psum.94 = f32[128]{0:T(128)S(1)} all-reduce(f32[128]{0:T(128)S(1)} %multiply_reduce_fusion), channel_id=1, replica_groups=mesh['sample'=4,'marker'=32] {'marker'}, use_global_device_ids=true, to_apply=%region_15.0 | all-reduce | flops 128 | bytes 1024 | tf_op jit(solution)/shard_map/psum | solution.py:60
  866.9 2.0 multiply_add_fusion
  868.9 0.0 copy-start.1
  868.9 1.3 copy-done.1
  870.3 0.0 copy-start.4
  870.3 0.0 copy-start.5
  870.3 0.0 copy-start.2
  870.3 0.3 fusion
  870.5 0.1 reshape.47
  870.7 66.8 %psum.95 = f32[16]{0:T(128)S(1)} all-reduce(f32[16]{0:T(128)S(1)} %reduce_sum.78), channel_id=1, replica_groups=mesh['sample'=4,'marker'=32] {'marker'}, use_global_device_ids=true, to_apply=%region_18.0 | all-reduce | flops 16 | bytes 128 | tf_op jit(solution)/shard_map/psum | solution.py:73
  937.5 0.0 copy-done.4
  937.5 0.0 copy-done.5
  937.5 0.0 copy-done.2
  937.5 2.0 fusion.16
  (11 shorter events, 0.1 us)
Async XLA Ops:
  7.2 181.9 %all-reduce.9.cloned.1.call-start = ((), (), s32[]{:S(2)}) async-start(), calls=%async_computation | async-start | bytes 262144 | tf_op jit(solution)/shard_map/psum | solution.py:24
  75.4 113.7 %copy-start.3 = (f32[16,2048]{1,0:T(8,128)S(1)}, f32[16,2048]{1,0:T(8,128)}, u32[]{:S(2)}) copy-start(f32[16,2048]{1,0:T(8,128)} %param.9) | copy-start | bytes 393220
  86.3 111.6 %copy-start.6 = (f32[16]{0:T(128)S(1)}, f32[16]{0:T(128)}, u32[]{:S(2)}) copy-start(f32[16]{0:T(128)} %param.15) | copy-start | bytes 196
  86.3 152.5 %copy-start = (f32[112,4096]{1,0:T(8,128)S(1)}, f32[112,4096]{1,0:T(8,128)}, u32[]{:S(2)}) copy-start(f32[112,4096]{1,0:T(8,128)} %param.11) | copy-start | bytes 5505028
  86.4 151.4 %all-reduce.11.cloned.1.call-start = ((), (), s32[]{:S(2)}) async-start(), calls=%async_computation.1 | async-start | bytes 524288 | tf_op jit(solution)/shard_map/psum | solution.py:47
  197.9 255.7 %all-reduce.13.cloned.1.call-start = ((), (), s32[]{:S(2)}) async-start(), calls=%async_computation.2 | async-start | bytes 4194304 | tf_op jit(solution)/shard_map/psum | solution.py:58
  393.9 407.5 %all-reduce.15.cloned.1.call-start = ((), (), s32[]{:S(2)}) async-start(), calls=%async_computation.3 | async-start | bytes 4194304 | tf_op jit(solution)/shard_map/psum | solution.py:58
  868.9 1.4 copy-start.1
  870.3 67.2 %copy-start.4 = (f32[16]{0:T(128)S(1)}, f32[16]{0:T(128)}, u32[]{:S(2)}) copy-start(f32[16]{0:T(128)} %param.13) | copy-start | bytes 196
  870.3 67.2 %copy-start.5 = (f32[16]{0:T(128)S(1)}, f32[16]{0:T(128)}, u32[]{:S(2)}) copy-start(f32[16]{0:T(128)} %param.14) | copy-start | bytes 196
  870.3 67.2 %copy-start.2 = (f32[16,4096]{1,0:T(8,128)S(1)}, f32[16,4096]{1,0:T(8,128)}, u32[]{:S(2)}) copy-start(f32[16,4096]{1,0:T(8,128)} %param.10) | copy-start | bytes 786436
Sparse Core Ops, SparseCore 0:
  86.5 102.5 all-reduce.8
  198.1 39.6 all-reduce.10
  394.0 59.5 all-reduce.12
  742.6 58.6 all-reduce.14
where the time goes:
time: 947 us; the launch traced here: 946 us
  blocking collectives  587 us (62%)
  waiting for transfers between devices  261 us (28%)
  matrix products  62.4 us (7%)
  other arithmetic  20.5 us (2%)
  between operations  13.9 us (1%)
    psum x2, blocking collectives, project(): predicted = lax.psum(partial_value, 'marker')  264 us
    psum x2, waiting for transfers between devices, per_device(): back_sum = lax.psum(back_sum, 'sample')  118 us
    psum x1, waiting for transfers between devices, project(): predicted = lax.psum(partial_value, 'marker')  103 us
    psum x1, blocking collectives, per_device(): norm_next = lax.psum(jnp.sum(residual * residual, axis=1), 'marker')  66.8 us
    psum x1, blocking collectives, per_device(): probe_dot = lax.psum(probe_local, 'marker')  66.8 us
    psum x1, blocking collectives, per_device(): first_slope = lax.psum(jnp.sum(slopes, axis=1), 'marker') / MARKERS  63.8 us
    psum x1, blocking collectives, per_device(): curvature = lax.psum(jnp.sum(direction * applied, axis=1), 'marker')  62.9 us
    psum x1, blocking collectives, per_device(): norm_start = lax.psum(jnp.sum(residual * residual, axis=1), 'marker')  62.9 us
  transfers between devices with their start and end apart: 4, of which 4 were waited for; matrix products, arithmetic and copies ran while one was open for 0% of the time, Pallas kernels for 0%

commit v1 on v0

--- a/solution.py
+++ b/solution.py
@@ -62,7 +62,9 @@
         iterate = iterate + step_size[:, None] * direction
         if iteration + 1 < ITERS:
             residual = residual - step_size[:, None] * applied
-            norm_next = lax.psum(jnp.sum(residual * residual, axis=1), "marker")
+            own = jnp.sum(residual * residual, axis=1)
+            parts = lax.all_gather(own, "marker", axis=0, tiled=False)
+            norm_next = parts.sum(axis=0)
             beta_ratio = norm_next / norm_now
             direction = residual + beta_ratio[:, None] * direction
             norm_now = norm_next

time: 947 us -> 904 us (0.955)
  blocking collectives: 587 us -> 544 us
    psum x1 -> x0, blocking collectives: 66.8 us -> none  [per_device(): norm_next = lax.psum(jnp.sum(residual * residual, axis=1), 'marker')]
    all_gather x0 -> x1, blocking collectives: none -> 22.1 us  [per_device(): parts = lax.all_gather(own, 'marker', axis=0, tiled=False)]
where the time goes in v1:
time: 904 us
  blocking collectives  544 us (60%)
  waiting for transfers between devices  261 us (29%)
  matrix products  62.4 us (7%)
  other arithmetic  20.5 us (2%)
  between operations  13.9 us (2%)
    psum x2, blocking collectives, project(): predicted = lax.psum(partial_value, 'marker')  266 us
    psum x2, waiting for transfers between devices, per_device(): back_sum = lax.psum(back_sum, 'sample')  118 us
    psum x1, waiting for transfers between devices, project(): predicted = lax.psum(partial_value, 'marker')  103 us
    psum x1, blocking collectives, per_device(): probe_dot = lax.psum(probe_local, 'marker')  66.8 us
    psum x1, blocking collectives, per_device(): first_slope = lax.psum(jnp.sum(slopes, axis=1), 'marker') / MARKERS  63.8 us
    psum x1, blocking collectives, per_device(): curvature = lax.psum(jnp.sum(direction * applied, axis=1), 'marker')  62.9 us
    psum x1, blocking collectives, per_device(): norm_start = lax.psum(jnp.sum(residual * residual, axis=1), 'marker')  62.9 us
    psum x1, waiting for transfers between devices, per_device(): start_back = lax.psum(start_back, 'sample')  39.8 us
  transfers between devices with their start and end apart: 4, of which 4 were waited for; matrix products, arithmetic and copies ran while one was open for 0% of the time, Pallas kernels for 0%

profile of v1, /device:TPU:1, one launch (start us, length us, event | category | flops | bytes accessed | tf_op | source)
XLA Modules:
  0.0 903.6 jit_solution(5767118933144338933)
XLA Ops:
  7.2 0.0 all-reduce.9.cloned.1.call-start
  7.2 0.7 multiply_add_fusion.4
  7.9 0.7 mul.192
  8.6 1.3 multiply_reduce_fusion.4
  9.8 63.8 %psum.77 = f32[16]{0:T(128)S(1)} all-reduce(f32[16]{0:T(128)S(1)} %multiply_reduce_fusion.4), channel_id=1, replica_groups=mesh['sample'=4,'marker'=32] {'marker'}, use_global_device_ids=true, to_apply=%region_1.0 | all-reduce | flops 16 | bytes 128 | tf_op jit(solution)/shard_map/psum | solution.py:43
  73.6 0.7 multiply_divide_fusion.1
  74.3 1.1 subtract_divide_fusion
  75.4 0.0 copy-start.3
  75.4 10.9 %fusion.17 = f32[16,2048]{1,0:T(8,128)} fusion(bf16[2048,4096]{1,0:T(8,128)(2,1)} %param.8, f32[16,4096]{1,0:T(8,128)S(1)} %subtract_divide_fusion), kind=kOutput, calls=%fused_computation.33 | convolution fusion | flops 268500992 | bytes 17170432 | tf_op jit(solution)/shard_map/dot_general | solution.py:17
  86.3 0.0 all-reduce.9.cloned.1.call-update
  86.3 0.0 copy-start.6
  86.3 0.0 copy-start
  86.4 0.0 all-reduce.11.cloned.1.call-start
  86.4 102.7 %all-reduce.9.cloned.1.call-done = f32[16,2048]{1,0:T(8,128)} async-done(((f32[16,2048]{1,0:T(8,128)}), f32[16,2048]{1,0:T(8,128)}) %all-reduce.9.cloned.1.call-update) | async-done | bytes 131088 | tf_op jit(solution)/shard_map/psum | solution.py:24
  189.1 0.0 copy-done.3
  189.1 8.8 fusion.19
  197.9 0.0 all-reduce.11.cloned.1.call-update
  197.9 0.0 all-reduce.13.cloned.1.call-start
  198.0 0.0 copy-done.6
  198.0 39.8 %all-reduce.11.cloned.1.call-done = f32[16,4096]{1,0:T(8,128)} async-done(((f32[16,4096]{1,0:T(8,128)}), f32[16,4096]{1,0:T(8,128)}) %all-reduce.11.cloned.1.call-update) | async-done | bytes 262160 | tf_op jit(solution)/shard_map/psum | solution.py:47
  237.8 1.0 broadcast_multiply_fusion
  238.8 0.0 copy-done
  238.8 11.4 %fusion.3 = f32[128,2048]{1,0:T(8,128)S(1)} fusion(bf16[2048,4096]{1,0:T(8,128)(2,1)} %param.8, f32[112,4096]{1,0:T(8,128)S(1)} %copy-done, f32[16,4096]{1,0:T(8,128)S(1)} %broadcast_multiply_fusion), kind=kOutput, calls=%fused_computation.13 | convolution fusion | flops 2149580800 | bytes 19922944 | tf_op jit(solution)/shard_map/dot_general | solution.py:17
  250.2 134.0 %all-reduce.16 = bf16[128,2048]{1,0:T(8,128)(2,1)} all-reduce(f32[128,2048]{1,0:T(8,128)S(1)} %fusion.3), channel_id=1, replica_groups=mesh['sample'=4,'marker'=32] {'marker'}, use_global_device_ids=true, to_apply=%region_6.0 | all-reduce | flops 262144 | bytes 1572864 | tf_op jit(solution)/shard_map/psum | solution.py:24
  384.2 9.6 %fusion.24 = f32[128,4096]{1,0:T(8,128)} fusion(bf16[128,2048]{1,0:T(8,128)(2,1)} %all-reduce.16, bf16[2048,4096]{1,0:T(8,128)(2,1)} %param.8), kind=kOutput, calls=%fused_computation.52 | convolution fusion | flops 2147483648 | bytes 19398656 | tf_op jit(solution)/shard_map/dot_general | solution.py:29
  393.9 0.0 all-reduce.13.cloned.1.call-update
  393.9 0.0 all-reduce.15.cloned.1.call-start
  394.0 0.1 mul.210
  394.0 0.1 mul.207
  394.1 59.5 %all-reduce.13.cloned.1.call-done = f32[128,4096]{1,0:T(8,128)} async-done(((f32[128,4096]{1,0:T(8,128)}), f32[128,4096]{1,0:T(8,128)}) %all-reduce.13.cloned.1.call-update) | async-done | bytes 2097168 | tf_op jit(solution)/shard_map/psum | solution.py:58
  453.6 2.2 multiply_reduce_fusion.2
  455.8 62.9 %all-reduce.1 = (f32[128]{0:T(128)S(1)}, f32[128]{0:T(128)S(1)}) all-reduce(f32[128]{0:T(128)S(1)} %get-tuple-element.3, f32[128]{0:T(128)S(1)} %get-tuple-element.2), channel_id=1, replica_groups=mesh['sample'=4,'marker'=32] {'marker'}, use_global_device_ids=true, to_apply=%region_5.0 | all-reduce | flops 256 | bytes 2048 | tf_op jit(solution)/shard_map/psum | solution.py:54
  518.7 2.2 multiply_reduce_fusion.1
  520.9 22.1 %all-gather.1 = f32[32,1,128]{2,1,0:T(1,128)S(1)} all-gather(f32[1,1,128]{2,1,0:T(1,128)S(1)} %bitcast.9), channel_id=2, replica_groups=mesh['sample'=4,'marker'=32] {'marker'}, dimensions={0}, use_global_device_ids=true | all-gather | bytes 16896 | tf_op jit(solution)/shard_map/all_gather | solution.py:66
  542.9 0.1 reduce_sum.85
  543.0 3.6 multiply_add_fusion.1
  546.6 12.1 %fusion.1 = f32[128,2048]{1,0:T(8,128)S(1)} fusion(bf16[2048,4096]{1,0:T(8,128)(2,1)} %param.8, f32[128,4096]{1,0:T(8,128)} %multiply_add_fusion.1), kind=kOutput, calls=%fused_computation.11 | convolution fusion | flops 2148007936 | bytes 19922944 | tf_op jit(solution)/shard_map/dot_general | solution.py:17
  558.7 131.8 %all-reduce.17 = bf16[128,2048]{1,0:T(8,128)(2,1)} all-reduce(f32[128,2048]{1,0:T(8,128)S(1)} %fusion.1), channel_id=1, replica_groups=mesh['sample'=4,'marker'=32] {'marker'}, use_global_device_ids=true, to_apply=%region_12.0 | all-reduce | flops 262144 | bytes 1572864 | tf_op jit(solution)/shard_map/psum | solution.py:24
  690.5 9.6 %fusion.23 = f32[128,4096]{1,0:T(8,128)} fusion(bf16[128,2048]{1,0:T(8,128)(2,1)} %all-reduce.17, bf16[2048,4096]{1,0:T(8,128)(2,1)} %param.8), kind=kOutput, calls=%fused_computation.51 | convolution fusion | flops 2147483648 | bytes 19398656 | tf_op jit(solution)/shard_map/dot_general | solution.py:29
  700.1 0.0 all-reduce.15.cloned.1.call-update
  700.1 0.1 slice.18
  700.2 0.1 reshape.48
  700.2 58.7 %all-reduce.15.cloned.1.call-done = f32[128,4096]{1,0:T(8,128)} async-done(((f32[128,4096]{1,0:T(8,128)}), f32[128,4096]{1,0:T(8,128)}) %all-reduce.15.cloned.1.call-update) | async-done | bytes 2097168 | tf_op jit(solution)/shard_map/psum | solution.py:58
  758.9 2.7 multiply_reduce_fusion
  761.6 62.9 %psum.86 = f32[128]{0:T(128)S(1)} all-reduce(f32[128]{0:T(128)S(1)} %multiply_reduce_fusion), channel_id=1, replica_groups=mesh['sample'=4,'marker'=32] {'marker'}, use_global_device_ids=true, to_apply=%region_15.0 | all-reduce | flops 128 | bytes 1024 | tf_op jit(solution)/shard_map/psum | solution.py:60
  824.5 2.0 multiply_add_fusion
  826.5 0.0 copy-start.1
  826.5 1.3 copy-done.1
  827.8 0.0 copy-start.4
  827.9 0.0 copy-start.5
  827.9 0.0 copy-start.2
  827.9 0.3 fusion
  828.1 0.1 reshape.47
  828.2 66.8 %psum.87 = f32[16]{0:T(128)S(1)} all-reduce(f32[16]{0:T(128)S(1)} %reduce_sum.88), channel_id=1, replica_groups=mesh['sample'=4,'marker'=32] {'marker'}, use_global_device_ids=true, to_apply=%region_18.0 | all-reduce | flops 16 | bytes 128 | tf_op jit(solution)/shard_map/psum | solution.py:75
  895.0 0.0 copy-done.4
  895.1 0.0 copy-done.5
  895.1 0.0 copy-done.2
  895.1 2.0 fusion.16
  (11 shorter events, 0.1 us)
Async XLA Ops:
  7.2 181.9 %all-reduce.9.cloned.1.call-start = ((), (), s32[]{:S(2)}) async-start(), calls=%async_computation | async-start | bytes 262144 | tf_op jit(solution)/shard_map/psum | solution.py:24
  75.4 113.7 %copy-start.3 = (f32[16,2048]{1,0:T(8,128)S(1)}, f32[16,2048]{1,0:T(8,128)}, u32[]{:S(2)}) copy-start(f32[16,2048]{1,0:T(8,128)} %param.9) | copy-start | bytes 393220
  86.3 111.6 %copy-start.6 = (f32[16]{0:T(128)S(1)}, f32[16]{0:T(128)}, u32[]{:S(2)}) copy-start(f32[16]{0:T(128)} %param.15) | copy-start | bytes 196
  86.3 152.5 %copy-start = (f32[112,4096]{1,0:T(8,128)S(1)}, f32[112,4096]{1,0:T(8,128)}, u32[]{:S(2)}) copy-start(f32[112,4096]{1,0:T(8,128)} %param.11) | copy-start | bytes 5505028
  86.4 151.4 %all-reduce.11.cloned.1.call-start = ((), (), s32[]{:S(2)}) async-start(), calls=%async_computation.1 | async-start | bytes 524288 | tf_op jit(solution)/shard_map/psum | solution.py:47
  197.9 255.7 %all-reduce.13.cloned.1.call-start = ((), (), s32[]{:S(2)}) async-start(), calls=%async_computation.2 | async-start | bytes 4194304 | tf_op jit(solution)/shard_map/psum | solution.py:58
  393.9 365.0 %all-reduce.15.cloned.1.call-start = ((), (), s32[]{:S(2)}) async-start(), calls=%async_computation.3 | async-start | bytes 4194304 | tf_op jit(solution)/shard_map/psum | solution.py:58
  826.5 1.4 copy-start.1
  827.8 67.2 %copy-start.4 = (f32[16]{0:T(128)S(1)}, f32[16]{0:T(128)}, u32[]{:S(2)}) copy-start(f32[16]{0:T(128)} %param.13) | copy-start | bytes 196
  827.9 67.2 %copy-start.5 = (f32[16]{0:T(128)S(1)}, f32[16]{0:T(128)}, u32[]{:S(2)}) copy-start(f32[16]{0:T(128)} %param.14) | copy-start | bytes 196
  827.9 67.2 %copy-start.2 = (f32[16,4096]{1,0:T(8,128)S(1)}, f32[16,4096]{1,0:T(8,128)}, u32[]{:S(2)}) copy-start(f32[16,4096]{1,0:T(8,128)} %param.10) | copy-start | bytes 786436
Sparse Core Ops, SparseCore 0:
  86.5 102.5 all-reduce.8
  198.1 39.6 all-reduce.10
  394.0 59.5 all-reduce.12
  700.2 58.6 all-reduce.14
